TPU v7x, 256 devices: a whole 4x4x8 slice. The times are simulated.
256 devices in a mesh: row: 16 (over z, core), col: 16 (over x, y).
Axes of the slice: x: 4, y: 4, z: 8, core: 2. Of those that a mesh axis runs over, the one named last changes fastest.
Arguments:
- gram: float32 [16, 16, 1024, 1024], P('row', 'col'), may hold values from -21834.348 to 21835.348, as said below
Outputs:
- factored: float32 [16, 16, 1024, 1024], P('row', 'col')
Inputs may be any that keep to these rules, and one draw needn't show every extreme that they name: gram holds a symmetric positive definite matrix of order 16384 whose smallest eigenvalue is at least 1.
All inputs are finite; a program needn't handle non-finite values.
Results may differ from a plain program's by a relative error of at most 0.0001.
Values sent between devices are 32-bit elements; how exact they have to be, the bound alone decides.
No kernel may reach another device: no remote copies, remote signals or barrier semaphores. Data moves between devices by JAX's collectives and lax.ppermute only.
A program may use at most 64 MiB of HBM per device.

v0:
```python
import jax
import jax.numpy as jnp
from jax import lax
from jax.sharding import Mesh
from jax.sharding import PartitionSpec as P

BS = 256
PANELS = 3
ROW = ("row_0", "row_1")


def broadcast(shard, axis, root):
    return lax.dynamic_index_in_dim(lax.all_gather(shard, axis), root, 0, keepdims=False)


def spread(shard, axis, root):
    mine = lax.axis_index(axis) == root
    return lax.psum(jnp.where(mine, shard, jnp.zeros_like(shard)), axis)


def rows_for(lines, devices):
    spare = -len(lines) % devices
    return jnp.pad(lines, [(0, spare)] + [(0, 0)] * (lines.ndim - 1))


def own_block(blocks, axes, sequence):
    inside = blocks.shape[1:]
    blocks = blocks.reshape(*(lax.axis_size(a) for a in axes), *inside)
    blocks = jnp.moveaxis(blocks, sequence, range(len(axes))).reshape(-1, *inside)
    for k in sequence:
        blocks = lax.psum_scatter(blocks, axes[k], scatter_dimension=0, tiled=True)
    return blocks[0]


def stacked_from(shard, axes, sequence):
    blocks = shard[None]
    for k in sequence:
        blocks = lax.all_gather(blocks, axes[k], axis=0, tiled=True)
    current = [lax.axis_size(axes[k]) for k in reversed(sequence)]
    blocks = blocks.reshape(*current, *shard.shape)
    turned = sorted(range(len(sequence)), key=lambda place: sequence[len(sequence) - 1 - place])
    return blocks.transpose(*turned, *range(len(sequence), blocks.ndim)).reshape(-1, *shard.shape)


def total_of(shard, axes, sequence):
    devices, lines = (lax.axis_size(axes), shard.reshape(-1, *shard.shape[1:][-1:]))
    blocks = rows_for(lines, devices).reshape(devices, -1, *lines.shape[1:])
    own = own_block(blocks, axes, sequence)
    whole = stacked_from(own, axes, sequence[::-1]).reshape(-1, *lines.shape[1:])
    return whole[: len(lines)].reshape(shard.shape)


def full_dot(left, right):
    return jnp.dot(
        left, right.T, precision=lax.Precision.HIGHEST, preferred_element_type=jnp.float32
    )


def on_device(gram):
    matrix = gram[0, 0]
    grid_rows = lax.axis_size(ROW)
    grid_cols = lax.axis_size("col")
    own_row = lax.axis_index(ROW)
    own_col = lax.axis_index("col")
    row_count = matrix.shape[0] // BS
    col_count = matrix.shape[1] // BS
    row_blocks = jnp.repeat(jnp.arange(row_count, dtype=jnp.int32) * grid_rows + own_row, BS)
    col_blocks = jnp.repeat(jnp.arange(col_count, dtype=jnp.int32) * grid_cols + own_col, BS)
    for step in range(PANELS):
        first = step // grid_cols * BS
        column = matrix[:, first : first + BS]
        factor_first = step // grid_rows * BS
        corner = broadcast(column[factor_first : factor_first + BS], ROW, step % grid_rows)
        holder = own_col == step % grid_cols
        corner = jnp.where(holder, corner, jnp.eye(BS, dtype=jnp.float32))
        diagonal = jnp.linalg.cholesky(corner)
        solved = lax.linalg.triangular_solve(
            diagonal, column, left_side=False, lower=True, transpose_a=True
        )
        tiled = jnp.tile(diagonal, (row_count, 1))
        result = jnp.where((row_blocks == step)[:, None], tiled, solved)
        result = jnp.where((row_blocks < step)[:, None], jnp.zeros_like(result), result)
        panel_rows = spread(result, "col", step % grid_cols)
        wanted = jnp.arange(col_count, dtype=jnp.int32)[:, None] * grid_cols + own_col
        summed_present = jnp.arange(row_count, dtype=jnp.int32)[None, :] * grid_rows + own_row
        select = (wanted == summed_present).astype(jnp.float32)
        pieces = jnp.einsum(
            "ci,irs->crs",
            select,
            panel_rows.reshape(row_count, BS, BS),
            precision=lax.Precision.HIGHEST,
        )
        panel_cols = total_of(pieces.reshape(col_count * BS, BS), ROW, (0, 1))
        left = jnp.where((row_blocks > step)[:, None], panel_rows, jnp.zeros_like(panel_rows))
        right = jnp.where((col_blocks > step)[:, None], panel_cols, jnp.zeros_like(panel_cols))
        current = matrix - full_dot(left, right)
        finish_first = step // grid_cols * BS
        present = current[:, finish_first : finish_first + BS]
        current = current.at[:, finish_first : finish_first + BS].set(
            jnp.where(own_col == step % grid_cols, panel_rows, present)
        )
        cleared = (row_blocks == step)[:, None] & (col_blocks > step)[None, :]
        matrix = jnp.where(cleared, jnp.zeros_like(current), current)
    return matrix[None, None]


def solution(mesh):
    split = Mesh(mesh.devices.reshape(8, 2, mesh.shape["col"]), ("row_0", "row_1", "col"))
    return jax.shard_map(
        on_device,
        mesh=split,
        in_specs=(P(ROW, "col", None, None),),
        out_specs=P(ROW, "col", None, None),
        check_vma=False,
    )
```

profile of v0, /device:TPU:84, one launch (start us, length us, event | category | flops | bytes accessed | tf_op | source)
XLA Modules:
  0.0 977.3 jit_solution(14150500300622532511)
XLA Ops:
  13.8 42.8 %all-gather.16.cloned.1.call-done = f32[4096,256]{0,1:T(8,128)} async-done(((f32[256,256]{0,1:T(8,128)}), f32[4096,256]{0,1:T(8,128)}) %all-gather.16.cloned.1.call-update) | async-done | bytes 4194320 | tf_op jit(solution)/shard_map/all_gather | solution.py:13
  58.7 11.7 %cholesky.172 = f32[128,128]{1,0:T(8,128)S(1)} custom-call(f32[128,128]{1,0:T(8,128)S(1)} %cholesky.270), custom_call_target="Cholesky" | custom-call | tf_op jit(solution)/shard_map/jit(cholesky)/cholesky | solution.py:76
  80.8 11.7 %cholesky.189 = f32[128,128]{1,0:T(8,128)S(1)} custom-call(f32[128,128]{1,0:T(8,128)S(1)} %convolution_subtract_fusion.8), custom_call_target="Cholesky" | custom-call | tf_op jit(solution)/shard_map/jit(cholesky)/cholesky | solution.py:76
  99.1 19.7 %custom-call.16 = f32[2,128,128]{1,2,0:T(8,128)S(1)} custom-call(f32[2,128,128]{2,1,0:T(8,128)S(1)} %get-tuple-element.63), custom_call_target="InvertDiagBlocksLowerTriangular" | custom-call | tf_op jit(solution)/shard_map/triangular_solve/custom-call.0 | solution.py:77
  124.6 95.1 %all-reduce.5.cloned.1.call-done = f32[1024,256]{0,1:T(8,128)} async-done(((f32[1024,256]{0,1:T(8,128)}), f32[1024,256]{0,1:T(8,128)}) %all-reduce.5.cloned.1.call-update) | async-done | bytes 1048592 | tf_op jit(solution)/shard_map/psum | solution.py:18
  224.5 38.6 %reduce-scatter.7.cloned.1.call-done = f32[2,64,256]{2,1,0:T(8,128)} async-done(((f32[16,64,256]{2,1,0:T(8,128)}), f32[2,64,256]{2,1,0:T(8,128)}) %reduce-scatter.7.cloned.1.call-update) | async-done | bytes 131088 | tf_op jit(solution)/shard_map/reduce_scatter | solution.py:31
  263.1 15.3 %reduce-scatter.9.cloned.1.call-done = f32[1,64,256]{2,1,0:T(8,128)} async-done(((f32[2,64,256]{2,1,0:T(8,128)}), f32[1,64,256]{2,1,0:T(8,128)}) %reduce-scatter.9.cloned.1.call-update) | async-done | bytes 65552 | tf_op jit(solution)/shard_map/reduce_scatter | solution.py:31
  282.9 37.7 %all-gather.10.cloned.1.call-done = f32[16,64,256]{2,1,0:T(8,128)} async-done(((f32[2,64,256]{2,1,0:T(8,128)}), f32[16,64,256]{2,1,0:T(8,128)}) %all-gather.10.cloned.1.call-update) | async-done | bytes 1048592 | tf_op jit(solution)/shard_map/all_gather | solution.py:38
  332.4 40.4 %all-gather.18.cloned.1.call-done = f32[4096,256]{0,1:T(8,128)} async-done(((f32[256,256]{0,1:T(8,128)}), f32[4096,256]{0,1:T(8,128)}) %all-gather.18.cloned.1.call-update) | async-done | bytes 4194320 | tf_op jit(solution)/shard_map/all_gather | solution.py:13
  375.0 11.7 %cholesky.206 = f32[128,128]{1,0:T(8,128)S(1)} custom-call(f32[128,128]{1,0:T(8,128)S(1)} %cholesky.273), custom_call_target="Cholesky" | custom-call | tf_op jit(solution)/shard_map/jit(cholesky)/cholesky | solution.py:76
  397.1 11.7 %cholesky.223 = f32[128,128]{1,0:T(8,128)S(1)} custom-call(f32[128,128]{1,0:T(8,128)S(1)} %convolution_subtract_fusion.7), custom_call_target="Cholesky" | custom-call | tf_op jit(solution)/shard_map/jit(cholesky)/cholesky | solution.py:76
  415.9 19.7 %custom-call.18 = f32[2,128,128]{1,2,0:T(8,128)S(1)} custom-call(f32[2,128,128]{2,1,0:T(8,128)S(1)} %get-tuple-element.64), custom_call_target="InvertDiagBlocksLowerTriangular" | custom-call | tf_op jit(solution)/shard_map/triangular_solve/custom-call.0 | solution.py:77
  441.4 95.1 %all-reduce.7.cloned.1.call-done = f32[1024,256]{0,1:T(8,128)} async-done(((f32[1024,256]{0,1:T(8,128)}), f32[1024,256]{0,1:T(8,128)}) %all-reduce.7.cloned.1.call-update) | async-done | bytes 1048592 | tf_op jit(solution)/shard_map/psum | solution.py:18
  541.4 38.6 %reduce-scatter.11.cloned.1.call-done = f32[2,64,256]{2,1,0:T(8,128)} async-done(((f32[16,64,256]{2,1,0:T(8,128)}), f32[2,64,256]{2,1,0:T(8,128)}) %reduce-scatter.11.cloned.1.call-update) | async-done | bytes 131088 | tf_op jit(solution)/shard_map/reduce_scatter | solution.py:31
  580.1 15.4 %reduce-scatter.13.cloned.1.call-done = f32[1,64,256]{2,1,0:T(8,128)} async-done(((f32[2,64,256]{2,1,0:T(8,128)}), f32[1,64,256]{2,1,0:T(8,128)}) %reduce-scatter.13.cloned.1.call-update) | async-done | bytes 65552 | tf_op jit(solution)/shard_map/reduce_scatter | solution.py:31
  599.3 38.3 %all-gather.12.cloned.1.call-done = f32[16,64,256]{2,1,0:T(8,128)} async-done(((f32[2,64,256]{2,1,0:T(8,128)}), f32[16,64,256]{2,1,0:T(8,128)}) %all-gather.12.cloned.1.call-update) | async-done | bytes 1048592 | tf_op jit(solution)/shard_map/all_gather | solution.py:38
  649.3 40.6 %all-gather.20.cloned.1.call-done = f32[4096,256]{0,1:T(8,128)} async-done(((f32[256,256]{0,1:T(8,128)}), f32[4096,256]{0,1:T(8,128)}) %all-gather.20.cloned.1.call-update) | async-done | bytes 4194320 | tf_op jit(solution)/shard_map/all_gather | solution.py:13
  692.1 11.7 %cholesky.240 = f32[128,128]{1,0:T(8,128)S(1)} custom-call(f32[128,128]{1,0:T(8,128)S(1)} %cholesky.276), custom_call_target="Cholesky" | custom-call | tf_op jit(solution)/shard_map/jit(cholesky)/cholesky | solution.py:76
  714.1 11.7 %cholesky.257 = f32[128,128]{1,0:T(8,128)S(1)} custom-call(f32[128,128]{1,0:T(8,128)S(1)} %convolution_subtract_fusion.6), custom_call_target="Cholesky" | custom-call | tf_op jit(solution)/shard_map/jit(cholesky)/cholesky | solution.py:76
  733.1 19.7 %custom-call.20 = f32[2,128,128]{1,2,0:T(8,128)S(1)} custom-call(f32[2,128,128]{2,1,0:T(8,128)S(1)} %get-tuple-element.65), custom_call_target="InvertDiagBlocksLowerTriangular" | custom-call | tf_op jit(solution)/shard_map/triangular_solve/custom-call.0 | solution.py:77
  758.6 95.1 %all-reduce.9.cloned.1.call-done = f32[1024,256]{0,1:T(8,128)} async-done(((f32[1024,256]{0,1:T(8,128)}), f32[1024,256]{0,1:T(8,128)}) %all-reduce.9.cloned.1.call-update) | async-done | bytes 1048592 | tf_op jit(solution)/shard_map/psum | solution.py:18
  858.5 38.6 %reduce-scatter.15.cloned.1.call-done = f32[2,64,256]{2,1,0:T(8,128)} async-done(((f32[16,64,256]{2,1,0:T(8,128)}), f32[2,64,256]{2,1,0:T(8,128)}) %reduce-scatter.15.cloned.1.call-update) | async-done | bytes 131088 | tf_op jit(solution)/shard_map/reduce_scatter | solution.py:31
  897.2 15.3 %reduce-scatter.17.cloned.1.call-done = f32[1,64,256]{2,1,0:T(8,128)} async-done(((f32[2,64,256]{2,1,0:T(8,128)}), f32[1,64,256]{2,1,0:T(8,128)}) %reduce-scatter.17.cloned.1.call-update) | async-done | bytes 65552 | tf_op jit(solution)/shard_map/reduce_scatter | solution.py:31
  916.2 38.4 %all-gather.14.cloned.1.call-done = f32[16,64,256]{2,1,0:T(8,128)} async-done(((f32[2,64,256]{2,1,0:T(8,128)}), f32[16,64,256]{2,1,0:T(8,128)}) %all-gather.14.cloned.1.call-update) | async-done | bytes 1048592 | tf_op jit(solution)/shard_map/all_gather | solution.py:38
  (191 shorter events, 156.7 us)
Async XLA Ops:
  6.5 50.1 %all-gather.16.cloned.1.call-start = ((), (), s32[]{:S(2)}) async-start(), calls=%async_computation.18 | async-start | bytes 4456448 | tf_op jit(solution)/shard_map/all_gather | solution.py:13
  13.6 206.1 %all-reduce.5.cloned.1.call-start = ((), (), s32[]{:S(2)}) async-start(), calls=%async_computation.6 | async-start | bytes 2097152 | tf_op jit(solution)/shard_map/psum | solution.py:18
  124.5 138.6 %reduce-scatter.7.cloned.1.call-start = ((), (), s32[]{:S(2)}) async-start(), calls=%async_computation.7 | async-start | bytes 1179648 | tf_op jit(solution)/shard_map/reduce_scatter | solution.py:31
  222.1 100.0 %copy-start.2 = (f32[1024,256]{0,1:T(8,128)S(1)}, f32[1024,256]{0,1:T(8,128)}, u32[]{:S(2)}) copy-start(f32[1024,256]{0,1:T(8,128)} %all-reduce.5.cloned.1.call-done) | copy-start | bytes 3145732
  224.5 54.0 %reduce-scatter.9.cloned.1.call-start = ((), (), s32[]{:S(2)}) async-start(), calls=%async_computation.8 | async-start | bytes 196608 | tf_op jit(solution)/shard_map/reduce_scatter | solution.py:31
  263.1 57.4 %all-gather.10.cloned.1.call-start = ((), (), s32[]{:S(2)}) async-start(), calls=%async_computation.9 | async-start | bytes 1179648 | tf_op jit(solution)/shard_map/all_gather | solution.py:38
  282.0 90.9 %all-gather.18.cloned.1.call-start = ((), (), s32[]{:S(2)}) async-start(), calls=%async_computation.19 | async-start | bytes 4456448 | tf_op jit(solution)/shard_map/all_gather | solution.py:13
  329.0 2.0 copy-start.1
  331.8 204.8 %all-reduce.7.cloned.1.call-start = ((), (), s32[]{:S(2)}) async-start(), calls=%async_computation.10 | async-start | bytes 2097152 | tf_op jit(solution)/shard_map/psum | solution.py:18
  441.4 138.6 %reduce-scatter.11.cloned.1.call-start = ((), (), s32[]{:S(2)}) async-start(), calls=%async_computation.11 | async-start | bytes 1179648 | tf_op jit(solution)/shard_map/reduce_scatter | solution.py:31
  539.0 100.2 %copy-start.4 = (f32[1024,256]{0,1:T(8,128)S(1)}, f32[1024,256]{0,1:T(8,128)}, u32[]{:S(2)}) copy-start(f32[1024,256]{0,1:T(8,128)} %all-reduce.7.cloned.1.call-done) | copy-start | bytes 3145732
  541.3 54.2 %reduce-scatter.13.cloned.1.call-start = ((), (), s32[]{:S(2)}) async-start(), calls=%async_computation.12 | async-start | bytes 196608 | tf_op jit(solution)/shard_map/reduce_scatter | solution.py:31
  580.0 57.6 %all-gather.12.cloned.1.call-start = ((), (), s32[]{:S(2)}) async-start(), calls=%async_computation.13 | async-start | bytes 1179648 | tf_op jit(solution)/shard_map/all_gather | solution.py:38
  599.0 90.9 %all-gather.20.cloned.1.call-start = ((), (), s32[]{:S(2)}) async-start(), calls=%async_computation.20 | async-start | bytes 4456448 | tf_op jit(solution)/shard_map/all_gather | solution.py:13
  646.1 2.0 copy-start
  648.8 204.8 %all-reduce.9.cloned.1.call-start = ((), (), s32[]{:S(2)}) async-start(), calls=%async_computation.14 | async-start | bytes 2097152 | tf_op jit(solution)/shard_map/psum | solution.py:18
  758.5 138.6 %reduce-scatter.15.cloned.1.call-start = ((), (), s32[]{:S(2)}) async-start(), calls=%async_computation.15 | async-start | bytes 1179648 | tf_op jit(solution)/shard_map/reduce_scatter | solution.py:31
  856.1 100.1 %copy-start.3 = (f32[1024,256]{0,1:T(8,128)S(1)}, f32[1024,256]{0,1:T(8,128)}, u32[]{:S(2)}) copy-start(f32[1024,256]{0,1:T(8,128)} %all-reduce.9.cloned.1.call-done) | copy-start | bytes 3145732
  858.5 54.0 %reduce-scatter.17.cloned.1.call-start = ((), (), s32[]{:S(2)}) async-start(), calls=%async_computation.16 | async-start | bytes 196608 | tf_op jit(solution)/shard_map/reduce_scatter | solution.py:31
  897.1 57.4 %all-gather.14.cloned.1.call-start = ((), (), s32[]{:S(2)}) async-start(), calls=%async_computation.17 | async-start | bytes 1179648 | tf_op jit(solution)/shard_map/all_gather | solution.py:38
Sparse Core Ops, SparseCore 0:
  13.7 42.8 all-gather.15
  124.6 94.9 all-reduce.4
  224.6 38.4 reduce-scatter.6
  265.4 13.0 reduce-scatter.8
  282.1 38.3 all-gather.9
  331.9 40.9 all-gather.17
  441.5 94.9 all-reduce.6
  541.4 38.4 reduce-scatter.10
  582.4 13.0 reduce-scatter.12
  599.2 38.3 all-gather.11
  649.0 40.9 all-gather.19
  758.6 94.9 all-reduce.8
  858.6 38.4 reduce-scatter.14
  899.4 13.0 reduce-scatter.16
  916.1 38.3 all-gather.13
where the time goes:
time: 989 us; the launch traced here: 977 us
  waiting for transfers between devices  686 us (69%)
  other arithmetic  179 us (18%)
  local copies, waits for them, and re-layouts  48.8 us (5%)
  matrix products  33 us (3%)
  between operations  18.3 us (2%)
  blocking collectives  10.5 us (1%)
    psum x3, waiting for transfers between devices, spread(): return lax.psum(jnp.where(mine, shard, jnp.zeros_like(shard)), axis)  285 us
    reduce_scatter x6, waiting for transfers between devices, own_block(): blocks = lax.psum_scatter(blocks, axes[k], scatter_dimension=0, tiled=True)  162 us
    all_gather x3, waiting for transfers between devices, broadcast(): lax.all_gather(shard, axis)  124 us
    all_gather x3, waiting for transfers between devices, stacked_from(): blocks = lax.all_gather(blocks, axes[k], axis=0, tiled=True)  114 us
    another operation x20, other arithmetic, on_device(): diagonal = jnp.linalg.cholesky(corner)  103 us
    another operation x7, other arithmetic, on_device(): lax.linalg.triangular_solve(diagonal, column, left_side=False, lower=True...  59.1 us
  transfers between devices with their start and end apart: 15, of which 15 were waited for; matrix products, arithmetic and copies ran while one was open for 0% of the time, Pallas kernels for 0%

commit v1 on v0

v1 whole, which is shorter than its diff:
```python
import jax
import jax.numpy as jnp
from jax import lax
from jax.experimental import pallas as pl
from jax.experimental.pallas import tpu as pltpu
from jax.sharding import Mesh
from jax.sharding import PartitionSpec as P

BS = 256
PANELS = 3
WIDTH = PANELS * BS
FACTOR = 128
ROW = ("row_0", "row_1")
COL = ("col_0", "col_1")
FULL = lax.Precision.HIGHEST
UPPER = ((0, 0), (0, 1), (0, 2), (1, 1), (1, 2), (2, 2))


def full_dot(left, right, dims):
    return lax.dot_general(
        left, right, (dims, ((), ())), precision=FULL, preferred_element_type=jnp.float32
    )


def factor_inverse(block):
    tiles = [block[8 * b : 8 * b + 8] for b in range(FACTOR // 8)]
    lane = lax.broadcasted_iota(jnp.int32, (8, FACTOR), 1)
    sub = lax.broadcasted_iota(jnp.int32, (8, FACTOR), 0)
    for k in range(FACTOR):
        first, s = divmod(k, 8)
        pivot = tiles[first][s : s + 1]
        scaled = jnp.where(lane[:1] == k, 1.0, pivot) * (1.0 / pivot[:, k : k + 1])
        for b in range(first, FACTOR // 8):
            tile = tiles[b]
            new = jnp.where(lane == k, 0.0, tile) - tile[:, k : k + 1] * scaled
            tiles[b] = jnp.where(sub > s, new, tile) if b == first else new
    rows = []
    for b, tile in enumerate(tiles):
        own = lane == sub + 8 * b
        pivots = jnp.sum(jnp.where(own, tile, 0.0), axis=1, keepdims=True)
        scale = lax.rsqrt(pivots)
        scale = scale * (1.5 - 0.5 * pivots * scale * scale)
        rows.append(jnp.where(lane < sub + 8 * b, tile * scale, jnp.where(own, scale, 0.0)))
    return jnp.concatenate(rows, axis=0)


def corner_kernel(corner, inverse, work):
    work[...] = jnp.zeros((WIDTH, WIDTH), jnp.float32)
    for n, (i, j) in enumerate(UPPER):
        work[i * BS : i * BS + BS, j * BS : j * BS + BS] = corner[:, n].reshape(BS, BS)
    for low in range(0, WIDTH, FACTOR):
        high = low + FACTOR
        own = factor_inverse(work[low:high, low:high])
        rows = full_dot(own, work[low:high, :], ((1,), (0,)))
        left = jnp.concatenate([rows[:, :low], own], axis=1) if low else own
        if high == WIDTH:
            inverse[low:high, :] = left
            break
        right = rows[:, high:]
        inverse[low:high, :] = jnp.concatenate([left, jnp.zeros_like(right)], axis=1)
        change = full_dot(right, jnp.concatenate([left, right], axis=1), ((0,), (0,)))
        if low:
            work[high:, :low] = work[high:, :low] - change[:, :low]
        work[high:, low:high] = -change[:, low:high]
        work[high:, high:] = work[high:, high:] - change[:, high:]


def corner_inverse(corner):
    return pl.pallas_call(
        corner_kernel,
        out_shape=jax.ShapeDtypeStruct((WIDTH, WIDTH), jnp.float32),
        scratch_shapes=[pltpu.VMEM((WIDTH, WIDTH), jnp.float32)],
        compiler_params=pltpu.CompilerParams(vmem_limit_bytes=56 << 20),
        name="corner",
    )(corner)


def solved(lines, inverse, store):
    for k in range(PANELS):
        total = None
        for j in range(k + 1):
            part = full_dot(lines[j], inverse[k * BS : k * BS + BS, j * BS : j * BS + BS], ((1,), (1,)))
            total = part if total is None else total + part
        store(k, total)


def panel_kernel(place, rows, cols, inverse, matrix, out, right, left):
    i = pl.program_id(0)
    own_row, own_col = place[0], place[1]
    count = matrix.shape[1] // BS

    @pl.when(i == 0)
    def _():
        for c in range(count):
            lines = [cols[4 * c : 4 * c + 4, k].reshape(BS, BS) for k in range(PANELS)]

            def keep(k, value, c=c):
                right[c * BS : c * BS + BS, k * BS : k * BS + BS] = value

            solved(lines, inverse, keep)

    def keep_left(k, value):
        left[:, k * BS : k * BS + BS] = value

    solved([rows[:, k].reshape(BS, BS) for k in range(PANELS)], inverse, keep_left)
    out[...] = matrix[...] - full_dot(left[...], right[...], ((1,), (1,)))
    block_row = i * 16 + own_row

    @pl.when(block_row < PANELS)
    def _():
        out[...] = jnp.zeros(out.shape, jnp.float32)

    for k in range(PANELS):

        @pl.when(own_col == k)
        def _(k=k):
            panel = left[:, k * BS : k * BS + BS]
            r = lax.broadcasted_iota(jnp.int32, (BS, BS), 0) + block_row * BS
            s = lax.broadcasted_iota(jnp.int32, (BS, BS), 1) + k * BS
            out[:, :BS] = jnp.where(r >= s, panel, 0.0)


def panel_update(place, rows, cols, inverse, matrix):
    size = matrix.shape[0]
    steps = size // BS
    pieces = rows.shape[0] // steps
    return pl.pallas_call(
        panel_kernel,
        grid_spec=pltpu.PrefetchScalarGridSpec(
            num_scalar_prefetch=1,
            grid=(steps,),
            in_specs=[
                pl.BlockSpec((pieces,) + rows.shape[1:], lambda i, _: (i, 0, 0, 0)),
                pl.BlockSpec(cols.shape, lambda i, _: (0, 0, 0, 0)),
                pl.BlockSpec(inverse.shape, lambda i, _: (0, 0)),
                pl.BlockSpec((BS, size), lambda i, _: (i, 0)),
            ],
            out_specs=pl.BlockSpec((BS, size), lambda i, _: (i, 0)),
            scratch_shapes=[
                pltpu.VMEM((size, WIDTH), jnp.float32),
                pltpu.VMEM((BS, WIDTH), jnp.float32),
            ],
        ),
        out_shape=jax.ShapeDtypeStruct(matrix.shape, jnp.float32),
        compiler_params=pltpu.CompilerParams(vmem_limit_bytes=56 << 20),
        name="panels",
    )(place, rows, cols, inverse, matrix)


def gathered(piece, axes):
    copies = jnp.broadcast_to(piece[None], (16,) + piece.shape)
    return lax.all_to_all(copies, axes, 0, 0, tiled=True)


def down_rows(piece):
    z = lax.axis_index("row_0")
    core = lax.axis_index("row_1")
    other = lax.ppermute(piece, "row_1", [(0, 1), (1, 0)])
    even = jnp.where(core == 0, piece, other)
    odd = jnp.where(core == 0, other, piece)
    met = lax.ppermute((even, odd), "row_0", [(0, 1), (1, 0)])
    near = z < 2
    first = jnp.where(z == 0, even, met[0])
    second = jnp.where(z == 0, odd, met[1])
    third = jnp.where(z == 0, met[0], even)
    have = jnp.stack([first, second, third])
    got = lax.ppermute(have, "row_0", [(0, 7), (1, 2)])
    have = jnp.where(near, have, got)
    got = lax.ppermute(have, "row_0", [(0, 6), (7, 5), (1, 3), (2, 4)])
    return jnp.where((z < 3) | (z == 7), have, got)


def on_device(gram):
    matrix = gram[0, 0]
    own_row = lax.axis_index(ROW)
    own_col = lax.axis_index(COL)
    place = jnp.stack([own_row, own_col]).astype(jnp.int32)
    top = matrix[:BS, :BS].reshape(16, 16, BS)
    top = lax.all_to_all(top, COL, 0, 0, tiled=True)[:PANELS]
    side = matrix[:, :BS].reshape(16, 64, BS)
    side = lax.all_to_all(side, COL, 0, 0, tiled=True)[:PANELS]
    lines = down_rows(top)
    corner = gathered(jnp.stack([lines[i, j] for i, j in UPPER]), COL)
    turned = lax.ppermute(side, ROW + COL, [(p * 16 + j, j * 16 + p) for p in range(16) for j in range(16)])
    rows = gathered(side, COL)
    cols = lax.all_gather(turned, ROW)
    inverse = corner_inverse(corner)
    return panel_update(place, rows, cols, inverse, matrix)[None, None]


def solution(mesh):
    split = Mesh(mesh.devices.reshape(8, 2, 4, 4), ROW + COL)
    return jax.shard_map(
        on_device,
        mesh=split,
        in_specs=(P(ROW, COL, None, None),),
        out_specs=P(ROW, COL, None, None),
        check_vma=False,
    )
```

time: 989 us -> 226 us (0.23)
  the two profiles are of different devices: /device:TPU:84 before, /device:TPU:8 now
where the time goes in v1:
time: 226 us; the launch traced here: 223 us
  Pallas kernels  103 us (46%)
  blocking collectives  57.3 us (25%)
  starting transfers between devices  27.9 us (12%)
  between operations  13.8 us (6%)
  waiting for transfers between devices  12.3 us (5%)
  local copies, waits for them, and re-layouts  7.87 us (3%)
    pallas_call x1, Pallas kernels, corner_inverse(): pl.pallas_call(corner_kernel, out_shape=jax.ShapeDtypeStruct((WIDTH, WIDT...  75.8 us
    all_to_all x1, blocking collectives, gathered(): return lax.all_to_all(copies, axes, 0, 0, tiled=True)  43 us
    pallas_call x1, Pallas kernels, panel_update(): pl.pallas_call(panel_kernel, grid_spec=pltpu.PrefetchScalarGridSpec(num_s...  26.8 us
    all_to_all x1, blocking collectives, on_device(): top = lax.all_to_all(top, COL, 0, 0, tiled=True)[:PANELS]  14.3 us
    ppermute x1, starting transfers between devices, down_rows(): got = lax.ppermute(have, 'row_0', [(0, 6), (7, 5), (1, 3), (2, 4)])  7.76 us
    all_to_all x1, waiting for transfers between devices, on_device(): side = lax.all_to_all(side, COL, 0, 0, tiled=True)[:PANELS]  6.32 us
    ppermute x2, starting transfers between devices, down_rows(): met = lax.ppermute((even, odd), 'row_0', [(0, 1), (1, 0)])  5.84 us
    all_to_all x1, starting transfers between devices, gathered(): return lax.all_to_all(copies, axes, 0, 0, tiled=True)  5.54 us
  transfers between devices with their start and end apart: 9, of which 4 were waited for; matrix products, arithmetic and copies ran while one was open for 2% of the time, Pallas kernels for 34%

profile of v1, /device:TPU:8, one launch (start us, length us, event | category | flops | bytes accessed | tf_op | source)
XLA Modules:
  0.0 222.5 jit_solution(1604743001008867864)
XLA Ops:
  6.5 1.0 slice.42
  7.5 14.3 %all_to_all.20 = f32[16,16,256]{2,1,0:T(8,128)S(1)} all-to-all(f32[16,16,256]{2,1,0:T(8,128)S(1)} %bitcast.41), channel_id=1, replica_groups=mesh['row_0'=8,'row_1'=2,'col_0'=4,'col_1'=4] {'col_0','col_1'}, dimensions={0} | all-to-all | bytes 524288 | tf_op jit(solution)/shard_map/all_to_all | solution.py:179
  21.8 2.3 %slice.40 = f32[1024,256]{1,0:T(8,128)} slice(f32[1024,1024]{1,0:T(8,128)} %bitcast.38), slice={[0:1024], [0:256]} | slice | bytes 2097152 | tf_op jit(solution)/shard_map/slice | solution.py:180
  24.0 5.1 %all-to-all-start = ((f32[16,64,256]{2,1,0:T(8,128)}), f32[16,64,256]{2,1,0:T(8,128)S(1)}, u32[]{:S(2)}, u32[]{:S(2)}) async-start(f32[16,64,256]{2,1,0:T(8,128)} %bitcast.3), calls=%async_computation | async-start | bytes 2097152 | tf_op jit(solution)/shard_map/all_to_all | solution.py:181
  29.1 0.0 all-gather.3.cloned.1.call-start
  29.2 3.8 %collective-permute-start.3 = (f32[3,16,256]{2,1,0:T(8,128)S(1)}, f32[3,16,256]{2,1,0:T(8,128)S(1)}, u32[]{:S(2)}, u32[]{:S(2)}) collective-permute-start(f32[3,16,256]{2,1,0:T(8,128)S(1)} %get-tuple-element.5), channel_id=1, source_target_pairs={{0,32},{32,0},{1,33},{33,1},{2,34},{34,2},{3,35},{35,3},{4,36},{36... | collective-permute-start | bytes 147464 | tf_op jit(solution)/shard_map/ppermute | solution.py:161
  33.0 2.0 collective-permute-start.2
  35.1 0.1 collective-permute-done.3
  35.2 3.8 %collective-permute-done.2 = f32[3,16,256]{2,1,0:T(8,128)S(1)} collective-permute-done((f32[3,16,256]{2,1,0:T(8,128)S(1)}, f32[3,16,256]{2,1,0:T(8,128)S(1)}, u32[]{:S(2)}, u32[]{:S(2)}) %collective-permute-start.2) | collective-permute-done | bytes 49184 | tf_op jit(solution)/shard_map/ppermute | solution.py:161
  39.1 1.3 collective-permute-start.4
  40.4 6.3 %all-to-all-done = f32[16,64,256]{2,1,0:T(8,128)S(1)} async-done(((f32[16,64,256]{2,1,0:T(8,128)}), f32[16,64,256]{2,1,0:T(8,128)S(1)}, u32[]{:S(2)}, u32[]{:S(2)}) %all-to-all-start) | async-done | bytes 1048608 | tf_op jit(solution)/shard_map/all_to_all | solution.py:181
  46.7 2.4 %collective-permute-start = (f32[3,64,256]{2,1,0:T(8,128)S(1)}, f32[3,64,256]{2,1,0:T(8,128)S(1)}, u32[]{:S(2)}, u32[]{:S(2)}) collective-permute-start(f32[3,64,256]{2,1,0:T(8,128)S(1)} %slice.41), channel_id=1, source_target_pairs={{0,0},{1,16},{2,32},{3,48},{4,64},{5,80},{6,96},{7,112},{8,128},{9... | collective-permute-start | bytes 589832 | tf_op jit(solution)/shard_map/ppermute | solution.py:184
  49.1 7.8 %collective-permute-start.5 = (f32[3,3,16,256]{3,2,1,0:T(8,128)S(1)}, f32[3,3,16,256]{3,2,1,0:T(8,128)S(1)}, u32[]{:S(2)}, u32[]{:S(2)}) collective-permute-start(f32[3,3,16,256]{3,2,1,0:T(8,128)S(1)} %broadcast_select_fusion), channel_id=1, source_target_pairs={{0,192},{224,160},{32,96},{64,128},{1,193},{225,161},{33,97},{65,1... | collective-permute-start | bytes 442376 | tf_op jit(solution)/shard_map/ppermute | solution.py:169
  56.9 0.7 copy-done.1
  57.6 0.0 all-gather.3.cloned.1.call-update
  57.6 2.0 collective-permute-done.5
  59.7 0.2 broadcast_in_dim.7
  59.9 43.0 %all_to_all.21.corner = f32[16,6,16,256]{3,2,1,0:T(8,128)} all-to-all(f32[16,6,16,256]{3,2,1,0:T(8,128)S(1)} %broadcast_in_dim.7), channel_id=1, replica_groups=mesh['row_0'=8,'row_1'=2,'col_0'=4,'col_1'=4] {'col_0','col_1'}, dimensions={0} | all-to-all | bytes 3145728 | tf_op jit(solution)/shard_map/all_to_all | solution.py:152
  102.9 2.0 broadcast_in_dim.6
  105.0 5.5 %all-to-all-start.1 = ((f32[16,3,64,256]{3,2,1,0:T(8,128)}), f32[16,3,64,256]{3,2,1,0:T(8,128)S(1)}, u32[]{:S(2)}, u32[]{:S(2)}) async-start(f32[16,3,64,256]{3,2,1,0:T(8,128)} %broadcast_in_dim.6), calls=%async_computation.1 | async-start | bytes 6291456 | tf_op jit(solution)/shard_map/all_to_all | solution.py:152
  110.5 0.6 pad_add_fusion.place
  111.2 75.8 %corner.1.inverse = f32[768,768]{1,0:T(8,128)} custom-call(f32[16,6,16,256]{3,2,1,0:T(8,128)} %all_to_all.21.corner), custom_call_target="tpu_custom_call" | custom-call | tf_op jit(solution)/shard_map/corner/pallas_call | solution.py:69
  187.0 1.7 copy-done
  188.7 26.8 %panels.1 = f32[1024,1024]{1,0:T(8,128)} custom-call(s32[2]{0:T(128)} %pad_add_fusion.place, f32[16,3,64,256]{3,2,1,0:T(8,128)} %copy-done, f32[16,3,64,256]{3,2,1,0:T(8,128)} %bitcast.40, f32[768,768]{1,0:T(8,128)} %corner.1.inverse, f32[1024,1024]{1,0:T(8,128)} %bitcast.39), custom_call_target="tpu_custom_call" | custom-call | tf_op jit(solution)/shard_map/panels/pallas_call | solution.py:127
  (22 shorter events, 0.2 us)
Async XLA Ops:
  21.8 7.4 %collective-permute-start.1 = (f32[3,16,256]{2,1,0:T(8,128)S(1)}, f32[3,16,256]{2,1,0:T(8,128)S(1)}, u32[]{:S(2)}, u32[]{:S(2)}) collective-permute-start(f32[3,16,256]{2,1,0:T(8,128)S(1)} %slice.43), channel_id=1, source_target_pairs={{0,16},{16,0},{1,17},{17,1},{2,18},{18,2},{3,19},{19,3},{4,20},{20... | collective-permute-start | bytes 147464 | tf_op jit(solution)/shard_map/ppermute | solution.py:158
  24.0 22.6 %all-to-all-start = ((f32[16,64,256]{2,1,0:T(8,128)}), f32[16,64,256]{2,1,0:T(8,128)S(1)}, u32[]{:S(2)}, u32[]{:S(2)}) async-start(f32[16,64,256]{2,1,0:T(8,128)} %bitcast.3), calls=%async_computation | async-start | bytes 2097152 | tf_op jit(solution)/shard_map/all_to_all | solution.py:181
  29.1 157.9 %all-gather.3.cloned.1.call-start = ((), (), s32[]{:S(2)}) async-start(), calls=%async_computation.4 | async-start | bytes 3342336 | tf_op jit(solution)/shard_map/all_gather | solution.py:186
  29.2 6.0 %collective-permute-start.3 = (f32[3,16,256]{2,1,0:T(8,128)S(1)}, f32[3,16,256]{2,1,0:T(8,128)S(1)}, u32[]{:S(2)}, u32[]{:S(2)}) collective-permute-start(f32[3,16,256]{2,1,0:T(8,128)S(1)} %get-tuple-element.5), channel_id=1, source_target_pairs={{0,32},{32,0},{1,33},{33,1},{2,34},{34,2},{3,35},{35,3},{4,36},{36... | collective-permute-start | bytes 147464 | tf_op jit(solution)/shard_map/ppermute | solution.py:161
  33.0 6.0 %collective-permute-start.2 = (f32[3,16,256]{2,1,0:T(8,128)S(1)}, f32[3,16,256]{2,1,0:T(8,128)S(1)}, u32[]{:S(2)}, u32[]{:S(2)}) collective-permute-start(f32[3,16,256]{2,1,0:T(8,128)S(1)} %get-tuple-element.6), channel_id=1, source_target_pairs={{0,32},{32,0},{1,33},{33,1},{2,34},{34,2},{3,35},{35,3},{4,36},{36... | collective-permute-start | bytes 147464 | tf_op jit(solution)/shard_map/ppermute | solution.py:161
  39.1 10.0 %collective-permute-start.4 = (f32[3,3,16,256]{3,2,1,0:T(8,128)S(1)}, f32[3,3,16,256]{3,2,1,0:T(8,128)S(1)}, u32[]{:S(2)}, u32[]{:S(2)}) collective-permute-start(f32[3,3,16,256]{3,2,1,0:T(8,128)S(1)} %pad_maximum_fusion), channel_id=1, source_target_pairs={{0,224},{32,64},{1,225},{33,65},{2,226},{34,66},{3,227},{35,67},{4... | collective-permute-start | bytes 442376 | tf_op jit(solution)/shard_map/ppermute | solution.py:167
  46.7 10.2 %collective-permute-start = (f32[3,64,256]{2,1,0:T(8,128)S(1)}, f32[3,64,256]{2,1,0:T(8,128)S(1)}, u32[]{:S(2)}, u32[]{:S(2)}) collective-permute-start(f32[3,64,256]{2,1,0:T(8,128)S(1)} %slice.41), channel_id=1, source_target_pairs={{0,0},{1,16},{2,32},{3,48},{4,64},{5,80},{6,96},{7,112},{8,128},{9... | collective-permute-start | bytes 589832 | tf_op jit(solution)/shard_map/ppermute | solution.py:184
  49.1 10.5 %collective-permute-start.5 = (f32[3,3,16,256]{3,2,1,0:T(8,128)S(1)}, f32[3,3,16,256]{3,2,1,0:T(8,128)S(1)}, u32[]{:S(2)}, u32[]{:S(2)}) collective-permute-start(f32[3,3,16,256]{3,2,1,0:T(8,128)S(1)} %broadcast_select_fusion), channel_id=1, source_target_pairs={{0,192},{224,160},{32,96},{64,128},{1,193},{225,161},{33,97},{65,1... | collective-permute-start | bytes 442376 | tf_op jit(solution)/shard_map/ppermute | solution.py:169
  56.9 0.7 copy-start.1
  105.0 82.0 %all-to-all-start.1 = ((f32[16,3,64,256]{3,2,1,0:T(8,128)}), f32[16,3,64,256]{3,2,1,0:T(8,128)S(1)}, u32[]{:S(2)}, u32[]{:S(2)}) async-start(f32[16,3,64,256]{3,2,1,0:T(8,128)} %broadcast_in_dim.6), calls=%async_computation.1 | async-start | bytes 6291456 | tf_op jit(solution)/shard_map/all_to_all | solution.py:152
  187.0 1.7 copy-start
Sparse Core Ops, SparseCore 0:
  57.8 56.2 all-gather.2
